TPU v7x, 128 devices: a whole 4x4x4 slice. The times are simulated.
128 devices in a mesh: view: 8 (over x, core), vox: 16 (over z, y).
Axes of the slice: x: 4, y: 4, z: 4, core: 2. Of those that a mesh axis runs over, the one named last changes fastest.
Arguments:
- features: bfloat16 [131072, 1024], P(('view', 'vox')), may hold values from -6 to 6
- w_embed: bfloat16 [1024, 768], replicated, may hold values from -0.1875 to 0.1875
- owner_device: int32 [131072, 1], P(('view', 'vox')), may hold values from 0 to 127; in each aligned block of 1024 rows (0 to 1023, 1024 to 2047, ...) at most 16 rows name the same one
- voxel_slot: int32 [131072], P(('view', 'vox')), may hold values from 0 to 511
- window_ids: int32 [65536], P(('view', 'vox')), may hold values from 0 to 1023, never falling along the last dimension, each value on 1 to 512 neighbouring positions
- w_heads: bfloat16 [768, 2304], replicated
- w_out: bfloat16 [768, 768], replicated, may hold values from -0.21875 to 0.21875
- w_up: bfloat16 [768, 3072], replicated, may hold values from -0.21875 to 0.21875
- w_down: bfloat16 [3072, 768], replicated, may hold values from -0.109375 to 0.109375
Outputs:
- encoded: bfloat16 [65536, 768], P(('view', 'vox'))
Inputs may be any that keep to these rules, and one draw needn't show every extreme that they name: `owner_device`: among the patches of one device, at most 16 name the same owner. `window_ids`: never falls along the voxels; a window is a run of 1 to 512 consecutive voxels.
All inputs are finite; a program needn't handle non-finite values.
Results may differ from a plain program's by a relative error of at most 0.013.
The roundings to bfloat16 on the way count: a program that leaves them out, or rounds other values in their place, can miss the bound.
Values may be sent and summed in bfloat16 or wider, within the bound.
No kernel may reach another device: no remote copies, remote signals or barrier semaphores. Data moves between devices by JAX's collectives and lax.ppermute only.
A program may use at most 128 MiB of HBM per device.

v0:
```python
import jax
import jax.numpy as jnp
from jax import lax
from jax.sharding import PartitionSpec as P

C = 768
HEADS = 12
WMOST = 512


epsilon = 1e-06


def passed_along(block, axis, distance):
    devices = range(lax.axis_size(axis))
    route = [(i - distance, i) for i in devices if i - distance in devices]
    return lax.ppermute(block, axis, route)


def layer_norm(values):
    average = jnp.mean(values, axis=-1, keepdims=True)
    centered = values - average
    variance = jnp.mean(centered * centered, axis=-1, keepdims=True)
    return centered * lax.rsqrt(variance + epsilon)


def local(features, w_embed, owner_device, voxel_slot, window_ids, w_heads, w_out, w_up, w_down):
    devices = lax.axis_size(("view", "vox"))
    patch_count = features.shape[0]
    voxels = window_ids.shape[0]
    capacity = max(2, 2 * patch_count // devices)
    target = owner_device[:, 0]
    owner_hits = (target[:, None] == jnp.arange(devices, dtype=jnp.int32)[None, :]).astype(
        jnp.int32
    )
    ranked = jnp.sum((jnp.cumsum(owner_hits, axis=0) - 1) * owner_hits, axis=1)
    position = target * capacity + ranked
    payload = jnp.dot(features, w_embed, preferred_element_type=jnp.float32).astype(jnp.bfloat16)
    buffer = (
        jnp.zeros((devices * capacity, payload.shape[1]), jnp.bfloat16).at[position].set(payload)
    )
    slot_buffer = jnp.full((devices * capacity,), -1, jnp.int32).at[position].set(voxel_slot)
    arrived, arrived_slot = (
        lax.all_to_all(
            buffer.reshape(devices, capacity, -1),
            ("view", "vox"),
            split_axis=0,
            concat_axis=0,
            tiled=True,
        ),
        lax.all_to_all(
            slot_buffer.reshape(devices, capacity),
            ("view", "vox"),
            split_axis=0,
            concat_axis=0,
            tiled=True,
        ),
    )
    arrived = arrived.reshape(devices * capacity, -1)
    arrived_slot = arrived_slot.reshape(devices * capacity)
    member = jnp.arange(voxels, dtype=jnp.int32)[:, None] == arrived_slot[None, :]
    summed = jnp.dot(member.astype(jnp.bfloat16), arrived, preferred_element_type=jnp.float32)
    counts = jnp.sum(member.astype(jnp.float32), axis=1, keepdims=True)
    latent = summed / jnp.maximum(counts, 1.0)
    normed = layer_norm(latent).astype(jnp.bfloat16)
    triple = jnp.dot(normed, w_heads, preferred_element_type=jnp.float32).astype(jnp.bfloat16)
    queries = triple[:, :C]
    key_value = triple[:, C:]
    window_tag = window_ids + 1
    rim_rows = WMOST
    before_kv, before_tag = passed_along((key_value, window_tag), ("view", "vox"), 1)
    after_kv, after_tag = passed_along((key_value, window_tag), ("view", "vox"), -1)
    keys_all = jnp.concatenate([before_kv, key_value, after_kv], axis=0)
    tags_all = jnp.concatenate([before_tag, window_tag, after_tag], axis=0)
    head_size = C // HEADS
    block_rows = min(512, voxels)
    slab_rows = block_rows + 2 * rim_rows

    def one_block(block_index):
        head_queries = queries.reshape(block_rows, HEADS, head_size)
        head_keys = keys_all[:, :C].reshape(slab_rows, HEADS, head_size)
        head_values = keys_all[:, C:].reshape(slab_rows, HEADS, head_size)
        scores = jnp.einsum(
            "qhd,khd->hqk", head_queries, head_keys, preferred_element_type=jnp.float32
        ) * head_size ** (-0.5)
        same = window_tag[:, None] == tags_all[None, :]
        scores = jnp.where(same[None], scores, -1e30)
        highest = jnp.max(scores, axis=-1, keepdims=True)
        exponent = jnp.exp(scores - highest)
        weights = (exponent / jnp.sum(exponent, axis=-1, keepdims=True)).astype(jnp.bfloat16)
        result = jnp.einsum(
            "hqk,khd->qhd", weights, head_values, preferred_element_type=jnp.float32
        )
        return result.reshape(block_rows, C).astype(jnp.bfloat16)

    attended = lax.map(one_block, jnp.arange(voxels // block_rows, dtype=jnp.int32)).reshape(
        voxels, C
    )
    middle = latent + jnp.dot(attended, w_out, preferred_element_type=jnp.float32)
    normed_two = layer_norm(middle).astype(jnp.bfloat16)
    expanded = jax.nn.gelu(
        jnp.dot(normed_two, w_up, preferred_element_type=jnp.float32), approximate=True
    ).astype(jnp.bfloat16)
    return (middle + jnp.dot(expanded, w_down, preferred_element_type=jnp.float32)).astype(
        jnp.bfloat16
    )


def solution(mesh):
    return jax.shard_map(
        local,
        mesh=mesh,
        in_specs=(
            P(("view", "vox"), None),
            P(),
            P(("view", "vox"), None),
            P(("view", "vox")),
            P(("view", "vox")),
            P(),
            P(),
            P(),
            P(),
        ),
        out_specs=P(("view", "vox"), None),
        check_vma=False,
    )
```

profile of v0, /device:TPU:5, one launch (start us, length us, event | category | flops | bytes accessed | tf_op | source)
XLA Modules:
  0.0 204.2 jit_solution(9374063384814307716)
XLA Ops:
  0.0 0.0 copy-start
  0.0 1.6 copy.25
  1.6 1.0 fusion.32
  2.6 0.0 copy-start.3
  2.6 0.8 copy-done.3
  3.5 1.1 add_add_fusion
  4.5 0.1 copy.26
  4.7 1.0 fusion.31
  5.7 0.0 copy-done.4
  5.7 4.5 %scatter_custom_fusion = s32[2048]{0:T(1024)S(1)} fusion(s32[1024]{0:T(1024)S(1)} %bitcast.51, s32[1024]{0:T(1024)} %param.12, s32[]{:T(128)} %constant.16.clone.1), kind=kCustom, calls=%fused_computation.55 | custom fusion | bytes 8704 | tf_op jit(solution)/shard_map/scatter | solution.py:42
  10.2 0.7 all_to_all.9
  10.9 11.3 %all-to-all-start = ((s32[128,1,16]{2,1,0:T(1,128)}), s32[128,1,16]{2,1,0:T(1,128)}, u32[]{:S(2)}, u32[]{:S(2)}) async-start(s32[128,1,16]{2,1,0:T(1,128)} %bitcast.47), calls=%async_computation | async-start | bytes 131072 | tf_op jit(solution)/shard_map/all_to_all | solution.py:51
  22.2 5.0 %convolution_convert_fusion.1 = bf16[1024,768]{1,0:T(8,128)(2,1)} fusion(bf16[1024,1024]{1,0:T(8,128)(2,1)} %param.9, bf16[1024,768]{1,0:T(8,128)(2,1)} %param.10), kind=kOutput, calls=%fused_computation.27 | convolution fusion | flops 1611399168 | bytes 5242880 | tf_op jit(solution)/shard_map/dot_general | solution.py:38
  27.2 7.9 %scatter_custom_fusion.1 = bf16[2048,768]{1,0:T(8,128)(2,1)} fusion(s32[1024]{0:T(1024)S(1)} %bitcast.52, bf16[1024,768]{1,0:T(8,128)(2,1)} %convolution_convert_fusion.1, bf16[]{:T(256)} %constant.20.clone.1), kind=kCustom, calls=%fused_computation.34 | custom fusion | bytes 3146240 | tf_op jit(solution)/shard_map/scatter | solution.py:40
  35.1 0.0 all-to-all-done
  35.1 10.2 %all-to-all-start.1 = ((bf16[128,16,768]{2,1,0:T(8,128)(2,1)}), bf16[128,16,768]{2,1,0:T(8,128)(2,1)}, u32[]{:S(2)}, u32[]{:S(2)}) async-start(bf16[128,16,768]{2,1,0:T(8,128)(2,1)} %bitcast.40), calls=%async_computation.1 | async-start | bytes 6291456 | tf_op jit(solution)/shard_map/all_to_all | solution.py:44
  45.3 0.5 broadcast.131
  45.8 2.2 %reduce.3 = s32[128,16]{1,0:T(8,128)} reduce(s32[128,1,16]{2,1,0:T(1,128)} %all-to-all-done, s32[]{:T(128)} %broadcast.131), dimensions={1}, to_apply=%all_to_all.10.reduce_sub_computation.3 | reduce | bytes 16388 | tf_op jit(solution)/shard_map/all_to_all | solution.py:51
  48.0 0.9 eq.73
  48.9 0.5 convert_reduce_fusion
  49.4 34.1 %all-to-all-done.1 = bf16[128,16,768]{2,1,0:T(8,128)(2,1)} async-done(((bf16[128,16,768]{2,1,0:T(8,128)(2,1)}), bf16[128,16,768]{2,1,0:T(8,128)(2,1)}, u32[]{:S(2)}, u32[]{:S(2)}) %all-to-all-start.1) | async-done | bytes 3145760 | tf_op jit(solution)/shard_map/all_to_all | solution.py:44
  83.5 3.9 %fusion.54 = (f32[512]{0:T(512)S(1)}, f32[512,768]{1,0:T(8,128)S(1)}) fusion(f32[512]{0:T(512)S(1)} %broadcast_maximum_fusion, bf16[2048,768]{1,0:T(8,128)(2,1)} %bitcast.9, s32[2048]{0:T(1024)S(1)} %eq.73), kind=kOutput, calls=%fused_computation.73 | convolution fusion | flops 1612447232 | bytes 4730880 | tf_op jit(solution)/shard_map/dot_general | solution.py:62
  87.4 0.3 multiply_reduce_fusion.1
  87.7 0.0 copy-done
  87.7 2.1 %convolution_convert_fusion = bf16[512,2304]{1,0:T(8,128)(2,1)S(1)} fusion(bf16[768,2304]{1,0:T(8,128)(2,1)S(1)} %copy-done, f32[512,768]{1,0:T(8,128)S(1)} %get-tuple-element.24, f32[512]{0:T(512)S(1)} %add_rsqrt_fusion.1, f32[512]{0:T(512)S(1)} %broadcast_multiply_fusion.1), kind=kOutput, calls=%fused_computation.21 | convolution fusion | flops 1814298624 | bytes 7475200 | tf_op jit(solution)/shard_map/dot_general | solution.py:66
  89.8 0.0 copy-start.5
  89.8 1.3 slice.28
  91.1 4.7 %collective-permute-start.1 = (bf16[512,1536]{1,0:T(8,128)(2,1)}, bf16[512,1536]{1,0:T(8,128)(2,1)}, u32[]{:S(2)}, u32[]{:S(2)}) collective-permute-start(bf16[512,1536]{1,0:T(8,128)(2,1)} %slice.28), channel_id=1, source_target_pairs={{1,0},{2,1},{3,2},{4,3},{5,4},{6,5},{7,6},{8,7},{9,8},{10,9},{11,1... | collective-permute-start | bytes 4718600 | tf_op jit(solution)/shard_map/ppermute | solution.py:17
  95.8 1.9 collective-permute-start
  97.8 7.0 %collective-permute-start.3 = (s32[512]{0:T(512)S(1)}, s32[512]{0:T(512)S(1)}, u32[]{:S(2)}, u32[]{:S(2)}) collective-permute-start(s32[512]{0:T(512)S(1)} %broadcast_add_fusion), channel_id=1, source_target_pairs={{1,0},{2,1},{3,2},{4,3},{5,4},{6,5},{7,6},{8,7},{9,8},{10,9},{11,1... | collective-permute-start | bytes 6152 | tf_op jit(solution)/shard_map/ppermute | solution.py:17
  104.7 1.9 collective-permute-start.2
  106.7 23.7 %collective-permute-done.3 = s32[512]{0:T(512)S(1)} collective-permute-done((s32[512]{0:T(512)S(1)}, s32[512]{0:T(512)S(1)}, u32[]{:S(2)}, u32[]{:S(2)}) %collective-permute-start.3) | collective-permute-done | bytes 2080 | tf_op jit(solution)/shard_map/ppermute | solution.py:17
  130.4 7.7 %collective-permute-done.2 = s32[512]{0:T(512)S(1)} collective-permute-done((s32[512]{0:T(512)S(1)}, s32[512]{0:T(512)S(1)}, u32[]{:S(2)}, u32[]{:S(2)}) %collective-permute-start.2) | collective-permute-done | bytes 2080 | tf_op jit(solution)/shard_map/ppermute | solution.py:17
  138.1 1.4 broadcast_compare_fusion
  139.5 0.9 slice.30
  140.4 2.4 %copy.29 = bf16[512,768]{0,1:T(8,128)(2,1)} copy(bf16[512,768]{1,0:T(8,128)(2,1)} %slice.30) | data formatting | bytes 1572864 | tf_op jit(solution)/shard_map/slice | solution.py:67
  142.8 0.0 collective-permute-done.1
  142.8 0.0 collective-permute-done
  142.8 2.5 %pad_maximum_fusion = bf16[1536,1536]{1,0:T(8,128)(2,1)S(1)} fusion(bf16[512,1536]{1,0:T(8,128)(2,1)} %collective-permute-done.1, bf16[512,1536]{1,0:T(8,128)(2,1)} %slice.28, bf16[512,1536]{1,0:T(8,128)(2,1)} %collective-permute-done), kind=kLoop, calls=%fused_computation.20 | loop fusion | flops 14155776 | bytes 9437184 | tf_op jit(solution)/shard_map/concatenate | solution.py:73
  145.3 2.5 %fusion.53 = (bf16[1536,768]{1,0:T(8,128)(2,1)}, bf16[1536,768]{1,0:T(8,128)(2,1)}) fusion(bf16[1536,1536]{1,0:T(8,128)(2,1)S(1)} %pad_maximum_fusion), kind=kLoop, calls=%fused_computation.72 | loop fusion | bytes 9437184 | tf_op jit(solution)/shard_map/while/body/eval_jaxpr/slice | solution.py:81
  147.8 4.3 %copy.30 = bf16[1536,768]{0,1:T(8,128)(2,1)} copy(bf16[1536,768]{1,0:T(8,128)(2,1)} %get-tuple-element.15) | data formatting | bytes 4718592 | tf_op jit(solution)/shard_map/while/body/eval_jaxpr/slice | solution.py:81
  152.1 4.3 %copy.28 = bf16[1536,768]{0,1:T(8,128)(2,1)} copy(bf16[1536,768]{1,0:T(8,128)(2,1)} %get-tuple-element.16) | data formatting | bytes 4718592 | tf_op jit(solution)/shard_map/while/body/eval_jaxpr/slice | solution.py:82
  156.4 14.7 %fusion.55 = f32[12,512]{1,0:T(8,128)} fusion(pred[512,1536]{1,0:T(8,128)(4,1)} %broadcast_compare_fusion, bf16[512,12,64]{0,2,1:T(8,128)(2,1)} %bitcast.45, bf16[1536,12,64]{0,2,1:T(8,128)(2,1)} %bitcast.41), kind=kOutput, calls=%fused_computation.74 | convolution fusion | flops 1245709824 | bytes 3956736 | tf_op jit(solution)/shard_map/while/body/eval_jaxpr/sub | solution.py:89
  171.1 17.9 %fusion.22 = bf16[12,64,512]{2,1,0:T(8,128)(2,1)} fusion(bf16[1536,12,64]{0,2,1:T(8,128)(2,1)} %bitcast.43, f32[12,512]{1,0:T(8,128)} %fusion.55, pred[512,1536]{1,0:T(8,128)(4,1)} %broadcast_compare_fusion, bf16[512,12,64]{0,2,1:T(8,128)(2,1)} %bitcast.46, bf16[1536,12,64]{0,2,1:T(8,128)(2,1)} %bitcast.42), kind=kOutput, calls=%fused_computation.37 | convolution fusion | flops 2463505920 | bytes 7102464 | tf_op jit(solution)/shard_map/while/body/eval_jaxpr/hqk,khd->qhd/dot_general | solution.py:91
  188.9 2.9 %fusion.56 = (f32[512]{0:T(512)S(1)}, f32[512,768]{1,0:T(8,128)S(1)}) fusion(f32[512,768]{1,0:T(8,128)} %copy-done.1, bf16[512,768]{0,1:T(8,128)(2,1)} %bitcast.44, bf16[768,768]{1,0:T(8,128)(2,1)} %param.15), kind=kOutput, calls=%fused_computation.75 | convolution fusion | flops 604765696 | bytes 5113856 | tf_op jit(solution)/shard_map/dot_general | solution.py:99
  191.8 1.1 copy-done.2
  193.0 0.3 multiply_reduce_fusion
  193.3 10.9 %add_convert_fusion = bf16[512,768]{1,0:T(8,128)(2,1)} fusion(f32[512,768]{1,0:T(8,128)} %copy-done.2, bf16[3072,768]{1,0:T(8,128)(2,1)} %param.17, bf16[768,3072]{1,0:T(8,128)(2,1)} %param.16, f32[512]{0:T(512)S(1)} %add_rsqrt_fusion, f32[512]{0:T(512)S(1)} %broadcast_multiply_fusion), kind=kOutput, calls=%fused_computation.28 | convolution fusion | flops 4847960064 | bytes 11800576 | tf_op jit(solution)/shard_map/dot_general | solution.py:104
  (16 shorter events, 0.1 us)
Async XLA Ops:
  0.0 87.7 %copy-start = (bf16[768,2304]{1,0:T(8,128)(2,1)S(1)}, bf16[768,2304]{1,0:T(8,128)(2,1)}, u32[]{:S(2)}) copy-start(bf16[768,2304]{1,0:T(8,128)(2,1)} %param.14) | copy-start | bytes 10616836
  0.0 5.7 %copy-start.4 = (s32[1024,1]{0,1:T(1,128)S(1)}, s32[1024,1]{0,1:T(1,128)}, u32[]{:S(2)}) copy-start(s32[1024,1]{0,1:T(1,128)} %param.11) | copy-start | bytes 12292
  2.6 0.8 copy-start.3
  10.9 24.2 %all-to-all-start = ((s32[128,1,16]{2,1,0:T(1,128)}), s32[128,1,16]{2,1,0:T(1,128)}, u32[]{:S(2)}, u32[]{:S(2)}) async-start(s32[128,1,16]{2,1,0:T(1,128)} %bitcast.47), calls=%async_computation | async-start | bytes 131072 | tf_op jit(solution)/shard_map/all_to_all | solution.py:51
  35.1 48.4 %all-to-all-start.1 = ((bf16[128,16,768]{2,1,0:T(8,128)(2,1)}), bf16[128,16,768]{2,1,0:T(8,128)(2,1)}, u32[]{:S(2)}, u32[]{:S(2)}) async-start(bf16[128,16,768]{2,1,0:T(8,128)(2,1)} %bitcast.40), calls=%async_computation.1 | async-start | bytes 6291456 | tf_op jit(solution)/shard_map/all_to_all | solution.py:44
  87.4 2.4 %copy-start.1 = (f32[512,768]{1,0:T(8,128)}, f32[512,768]{1,0:T(8,128)S(1)}, u32[]{:S(2)}) copy-start(f32[512,768]{1,0:T(8,128)S(1)} %get-tuple-element.24) | copy-start | bytes 4718596
  89.8 7.9 %copy-start.5 = (s32[512]{0:T(512)S(1)}, s32[512]{0:T(512)}, u32[]{:S(2)}) copy-start(s32[512]{0:T(512)} %param.13) | copy-start | bytes 6148
  91.1 51.7 %collective-permute-start.1 = (bf16[512,1536]{1,0:T(8,128)(2,1)}, bf16[512,1536]{1,0:T(8,128)(2,1)}, u32[]{:S(2)}, u32[]{:S(2)}) collective-permute-start(bf16[512,1536]{1,0:T(8,128)(2,1)} %slice.28), channel_id=1, source_target_pairs={{1,0},{2,1},{3,2},{4,3},{5,4},{6,5},{7,6},{8,7},{9,8},{10,9},{11,1... | collective-permute-start | bytes 4718600 | tf_op jit(solution)/shard_map/ppermute | solution.py:17
  95.8 47.0 %collective-permute-start = (bf16[512,1536]{1,0:T(8,128)(2,1)}, bf16[512,1536]{1,0:T(8,128)(2,1)}, u32[]{:S(2)}, u32[]{:S(2)}) collective-permute-start(bf16[512,1536]{1,0:T(8,128)(2,1)} %slice.28), channel_id=1, source_target_pairs={{0,1},{1,2},{2,3},{3,4},{4,5},{5,6},{6,7},{7,8},{8,9},{9,10},{10,1... | collective-permute-start | bytes 4718600 | tf_op jit(solution)/shard_map/ppermute | solution.py:17
  97.8 32.6 %collective-permute-start.3 = (s32[512]{0:T(512)S(1)}, s32[512]{0:T(512)S(1)}, u32[]{:S(2)}, u32[]{:S(2)}) collective-permute-start(s32[512]{0:T(512)S(1)} %broadcast_add_fusion), channel_id=1, source_target_pairs={{1,0},{2,1},{3,2},{4,3},{5,4},{6,5},{7,6},{8,7},{9,8},{10,9},{11,1... | collective-permute-start | bytes 6152 | tf_op jit(solution)/shard_map/ppermute | solution.py:17
  104.7 33.3 %collective-permute-start.2 = (s32[512]{0:T(512)S(1)}, s32[512]{0:T(512)S(1)}, u32[]{:S(2)}, u32[]{:S(2)}) collective-permute-start(s32[512]{0:T(512)S(1)} %broadcast_add_fusion), channel_id=1, source_target_pairs={{0,1},{1,2},{2,3},{3,4},{4,5},{5,6},{6,7},{7,8},{8,9},{9,10},{10,1... | collective-permute-start | bytes 6152 | tf_op jit(solution)/shard_map/ppermute | solution.py:17
  191.8 1.2 copy-start.2
where the time goes:
time: 205 us; the launch traced here: 204 us
  waiting for transfers between devices  65.5 us (32%)
  matrix products  57.2 us (28%)
  starting transfers between devices  37 us (18%)
  local copies, waits for them, and re-layouts  33.8 us (16%)
  other arithmetic  10.4 us (5%)
    all_to_all x1, waiting for transfers between devices, local(): lax.all_to_all(buffer.reshape(devices, capacity, -1), ('view', 'vox'), sp...  34.1 us
    ppermute x4, waiting for transfers between devices, passed_along(): return lax.ppermute(block, axis, route)  31.4 us
    dot_general x1, matrix products, one_block(): jnp.einsum('hqk,khd->qhd', weights, head_values, preferred_element_type=j...  17.9 us
    ppermute x4, starting transfers between devices, passed_along(): return lax.ppermute(block, axis, route)  15.5 us
    sub x1, matrix products, one_block(): exponent = jnp.exp(scores - highest)  14.7 us
    all_to_all x1, starting transfers between devices, local(): lax.all_to_all(slot_buffer.reshape(devices, capacity), ('view', 'vox'), s...  11.3 us
    dot_general x1, matrix products, local(): jnp.dot(expanded, w_down, preferred_element_type=jnp.float32)  10.9 us
    all_to_all x1, starting transfers between devices, local(): lax.all_to_all(buffer.reshape(devices, capacity, -1), ('view', 'vox'), sp...  10.2 us
  transfers between devices with their start and end apart: 6, of which 3 were waited for; matrix products, arithmetic and copies ran while one was open for 11% of the time, Pallas kernels for 0%

commit v1 on v0

v1 whole, which is shorter than its diff:
```python
import jax
import jax.numpy as jnp
from jax import lax
from jax.experimental import pallas as pl
from jax.experimental.pallas import tpu as pltpu
from jax.sharding import PartitionSpec as P

C = 768
HEADS = 12
HEAD = C // HEADS
PAIRS = HEADS // 2
LANES = 128
CHUNKS = C // LANES
BLOCK = 128
epsilon = 1e-06
AXES = ("view", "vox")
f32 = jnp.float32
bf16 = jnp.bfloat16
i32 = jnp.int32
MASKED = -1e30


def passed_along(block, distance):
    devices = range(lax.axis_size(AXES))
    route = [(i - distance, i) for i in devices if i - distance in devices]
    return lax.ppermute(block, AXES, route)


def layer_norm(values):
    average = jnp.mean(values, axis=-1, keepdims=True)
    centered = values - average
    variance = jnp.mean(centered * centered, axis=-1, keepdims=True)
    return centered * lax.rsqrt(variance + epsilon)


def across(a, b):
    return lax.dot_general(a, b, (((1,), (1,)), ((), ())), preferred_element_type=f32)


def dot(a, b):
    return jnp.dot(a, b, preferred_element_type=f32)


def iota(shape, dim):
    return lax.broadcasted_iota(i32, shape, dim)


def params(mib):
    return pltpu.CompilerParams(vmem_limit_bytes=mib << 20)


def dispatch_kernel(
    features_ref, embed_ref, owner_ref, slot_ref, out_ref, payload_ref, position_ref, digits_ref
):
    step = pl.program_id(0)
    patches = features_ref.shape[0]
    devices = digits_ref.shape[1]
    group = out_ref.shape[0]
    capacity = (out_ref.shape[1] - 8) // CHUNKS
    part = 256
    mine = lax.rem(lax.axis_index("vox"), LANES // capacity)

    @pl.when(step == 0)
    def _():
        owner = owner_ref[...]
        hits = jnp.where(iota((devices, patches), 0) == owner, 1.0, 0.0)
        earlier = jnp.where(iota((part, part), 0) < iota((part, part), 1), 1.0, 0.0).astype(bf16)
        running = jnp.zeros((devices, 1), f32)
        ranks = []
        for start in range(0, patches, part):
            here = hits[:, start : start + part]
            before = dot(here.astype(bf16), earlier) + running
            running = running + jnp.sum(here, axis=1, keepdims=True)
            ranks.append(jnp.sum(here * before, axis=0, keepdims=True))
        rank = jnp.concatenate(ranks, axis=1).astype(i32)
        position_ref[...] = owner * capacity + rank
        place = jnp.where(iota((LANES, patches), 0) == rank + capacity * mine, 1.0, 0.0).astype(bf16)
        code = slot_ref[...] + 1
        high = (code >> 4).astype(f32)
        low = (code & 15).astype(f32)
        digits_ref[0] = across((hits * high).astype(bf16), place)
        digits_ref[1] = across((hits * low).astype(bf16), place)
        payload_ref[...] = dot(features_ref[...], embed_ref[...]).astype(bf16)

    rows = group * capacity
    chosen = jnp.where(iota((rows, patches), 0) + step * rows == position_ref[...], 1.0, 0.0)
    block = dot(chosen.astype(bf16), payload_ref[...]).astype(bf16)
    for c in range(CHUNKS):
        out_ref[:, c * capacity : (c + 1) * capacity, :] = block[
            :, c * LANES : (c + 1) * LANES
        ].reshape(group, capacity, LANES)
    here = pl.ds(pl.multiple_of(step * group, 8), group)
    high = jnp.broadcast_to(digits_ref[0, here, :][:, None, :], (group, 8, LANES))
    low = jnp.broadcast_to(digits_ref[1, here, :][:, None, :], (group, 8, LANES))
    out_ref[:, CHUNKS * capacity :, :] = jnp.where(
        iota((group, 8, LANES), 1) < 4, high, low
    ).astype(bf16)


def dispatch(features, w_embed, owner, slot, devices, capacity):
    patches, width = features.shape
    group = 32
    tall = CHUNKS * capacity + 8
    whole = lambda i: (0, 0)
    return pl.pallas_call(
        dispatch_kernel,
        out_shape=jax.ShapeDtypeStruct((devices, tall, LANES), bf16),
        grid=(devices // group,),
        in_specs=[
            pl.BlockSpec((patches, width), whole, pipeline_mode=pl.Buffered(1)),
            pl.BlockSpec((width, C), whole, pipeline_mode=pl.Buffered(1)),
            pl.BlockSpec((1, patches), whole),
            pl.BlockSpec((1, patches), whole),
        ],
        out_specs=pl.BlockSpec((group, tall, LANES), lambda i: (i, 0, 0)),
        scratch_shapes=[
            pltpu.VMEM((patches, C), bf16),
            pltpu.VMEM((1, patches), i32),
            pltpu.VMEM((2, devices, LANES), f32),
        ],
        compiler_params=params(24),
        name="dispatch",
    )(features, w_embed, owner, slot)


def gather_kernel(arrived_ref, latent_ref, normed_ref, total_ref, tally_ref):
    step = pl.program_id(0)
    sources = arrived_ref.shape[0]
    capacity = (arrived_ref.shape[1] - 8) // CHUNKS
    voxels = latent_ref.shape[0]
    each = LANES // capacity
    digits = arrived_ref[:, CHUNKS * capacity :, :].astype(f32)
    digits = jnp.sum(digits.reshape(sources // each, each, 8, LANES), axis=1)
    code = digits[:, 0, :] * 16.0 + digits[:, 4, :]
    slot = jnp.concatenate([code[g : g + 1] for g in range(sources // each)], axis=1).astype(i32) - 1
    rows = sources * capacity
    member = jnp.where(iota((voxels, rows), 0) == slot, 1.0, 0.0)
    data = jnp.concatenate(
        [
            arrived_ref[:, c * capacity : (c + 1) * capacity, :].reshape(rows, LANES)
            for c in range(CHUNKS)
        ],
        axis=1,
    )
    added = dot(member.astype(bf16), data)
    counted = member[:, :LANES]
    for k in range(1, rows // LANES):
        counted = counted + member[:, k * LANES : (k + 1) * LANES]

    @pl.when(step == 0)
    def _():
        total_ref[...] = added
        tally_ref[...] = counted

    @pl.when(step > 0)
    def _():
        total_ref[...] += added
        tally_ref[...] += counted

    @pl.when(step == pl.num_programs(0) - 1)
    def _():
        counts = jnp.sum(tally_ref[...], axis=1, keepdims=True)
        latent = total_ref[...] / jnp.maximum(counts, 1.0)
        latent_ref[...] = latent
        normed_ref[...] = layer_norm(latent).astype(bf16)


def gather(arrived, voxels):
    sources, tall, _ = arrived.shape
    group = 32
    whole = lambda i: (0, 0)
    return pl.pallas_call(
        gather_kernel,
        out_shape=(
            jax.ShapeDtypeStruct((voxels, C), f32),
            jax.ShapeDtypeStruct((voxels, C), bf16),
        ),
        grid=(sources // group,),
        in_specs=[pl.BlockSpec((group, tall, LANES), lambda i: (i, 0, 0))],
        out_specs=(pl.BlockSpec((voxels, C), whole), pl.BlockSpec((voxels, C), whole)),
        scratch_shapes=[pltpu.VMEM((voxels, C), f32), pltpu.VMEM((voxels, LANES), f32)],
        compiler_params=params(20),
        name="gather",
    )(arrived)


def column_of(row):
    return jnp.broadcast_to(row, (LANES, row.shape[1])).T


def by_half(first, second):
    return jnp.where(iota(first.shape, 1) < HEAD, first, second)


def scores_of(query_pair, key_pair, half, bias):
    lane = iota(query_pair.shape, 1)
    keep = (lane >= HEAD) if half else (lane < HEAD)
    return across(jnp.where(keep, query_pair, jnp.zeros_like(query_pair)), key_pair) + bias


def weighted(score, highest, value_pair):
    exponent = jnp.exp(score - highest).astype(bf16)
    wide = jnp.concatenate([value_pair, jnp.ones_like(value_pair)], axis=1)
    return dot(exponent, wide)


def bias_of(column, row):
    tiles = [
        jnp.where(column == row[:, k : k + LANES], 0.0, MASKED) for k in range(0, row.shape[1], LANES)
    ]
    return jnp.concatenate(tiles, axis=1)


def near_kernel(
    tag_ref, tag_row_ref, normed_ref, heads_ref, query_ref, value_ref, top_ref, sum_ref, kv_ref, column_ref
):
    voxels = normed_ref.shape[0]
    blocks = voxels // BLOCK
    normed = normed_ref[...]
    query_ref[...] = dot(normed, heads_ref[:, :C]).astype(bf16) * jnp.asarray(HEAD**-0.5, bf16)
    kv_ref[...] = dot(normed, heads_ref[:, C:]).astype(bf16)
    column_ref[...] = column_of(tag_row_ref[...])

    def one_block(b, carry):
        rows = pl.ds(pl.multiple_of(b * BLOCK, BLOCK), BLOCK)
        first, last = tag_ref[b * BLOCK], tag_ref[b * BLOCK + BLOCK - 1]
        low = i32(0)
        high = i32(0)
        for k in range(blocks):
            low = low + (tag_ref[k * BLOCK + BLOCK - 1] < first).astype(i32)
            high = high + (tag_ref[k * BLOCK] <= last).astype(i32)
        count = high - low

        def attend(n):
            keys = pl.ds(pl.multiple_of(low * BLOCK, BLOCK), n * BLOCK)
            bias = bias_of(column_ref[rows, :], tag_row_ref[:, keys])
            for p in range(PAIRS):
                lanes = slice(p * LANES, (p + 1) * LANES)
                query = query_ref[rows, lanes]
                key = kv_ref[keys, lanes]
                value = kv_ref[keys, C + p * LANES : C + (p + 1) * LANES]
                outs, tops = [], []
                for half in range(2):
                    score = scores_of(query, key, half, bias)
                    highest = jnp.max(score, axis=1, keepdims=True)
                    outs.append(weighted(score, highest, value))
                    tops.append(jnp.broadcast_to(highest, (BLOCK, LANES)))
                value_ref[rows, lanes] = by_half(outs[0][:, :LANES], outs[1][:, :LANES])
                sum_ref[rows, lanes] = by_half(outs[0][:, LANES:], outs[1][:, LANES:])
                top_ref[rows, lanes] = by_half(tops[0], tops[1])

        for n in range(1, blocks + 1):
            pl.when(count == n)(lambda n=n: attend(n))
        return carry

    lax.fori_loop(0, blocks, one_block, 0)


VMEM = pl.BlockSpec(memory_space=pltpu.VMEM)
SMEM = pl.BlockSpec(memory_space=pltpu.SMEM)


def near(tags, normed, w_heads):
    voxels = normed.shape[0]
    return pl.pallas_call(
        near_kernel,
        out_shape=(
            jax.ShapeDtypeStruct((voxels, C), bf16),
            jax.ShapeDtypeStruct((voxels, C), f32),
            jax.ShapeDtypeStruct((voxels, C), f32),
            jax.ShapeDtypeStruct((voxels, C), f32),
        ),
        in_specs=[SMEM, VMEM, VMEM, VMEM],
        out_specs=(VMEM, VMEM, VMEM, VMEM),
        scratch_shapes=[pltpu.VMEM((voxels, 2 * C), bf16), pltpu.VMEM((voxels, LANES), i32)],
        compiler_params=params(20),
        name="near",
    )(tags, tags.reshape(1, voxels), normed, w_heads)


def finish_kernel(
    tag_ref, before_tag_ref, after_tag_ref, tag_row_ref, before_row_ref, after_row_ref,
    before_ref, after_ref, heads_ref, query_ref, near_value_ref, near_top_ref, near_sum_ref, latent_ref,
    w_out_ref, w_up_ref, w_down_ref, out_ref, kv_ref, column_ref, row_ref, value_ref, top_ref, sum_ref
):
    voxels = query_ref.shape[0]
    blocks = voxels // BLOCK
    sizes = (2, blocks)
    value_ref[...] = near_value_ref[...]
    top_ref[...] = near_top_ref[...]
    sum_ref[...] = near_sum_ref[...]
    column_ref[...] = column_of(tag_row_ref[...])
    start_tag, end_tag = tag_ref[0], tag_ref[voxels - 1]
    before_count = i32(0)
    after_count = i32(0)
    for k in range(blocks):
        before_count += (before_tag_ref[k * BLOCK + BLOCK - 1] == start_tag).astype(i32)
        after_count += (after_tag_ref[k * BLOCK] == end_tag).astype(i32)

    def project(side, source_ref, source_row_ref, n):
        size = n * BLOCK
        start = 0 if side else voxels - size
        kv_ref[side, :size] = dot(source_ref[start : start + size, :], heads_ref[:, C:]).astype(bf16)
        row_ref[side, :, :size] = source_row_ref[:, start : start + size]

    def span(count, action):
        for lower, n in zip((0,) + sizes, sizes):
            pl.when(jnp.logical_and(count > lower, count <= n))(lambda n=n: action(n))

    span(before_count, lambda n: project(0, before_ref, before_row_ref, n))
    span(after_count, lambda n: project(1, after_ref, after_row_ref, n))

    def one_block(step, carry):
        side, b = step // blocks, step % blocks
        rows = pl.ds(pl.multiple_of(b * BLOCK, BLOCK), BLOCK)
        touched = jnp.where(
            side == 0, tag_ref[b * BLOCK] == start_tag, tag_ref[b * BLOCK + BLOCK - 1] == end_tag
        )
        count = jnp.where(touched, jnp.where(side == 0, before_count, after_count), 0)

        def attend(n):
            size = n * BLOCK
            bias = bias_of(column_ref[rows, :], row_ref[side, :, :size])
            for p in range(PAIRS):
                lanes = slice(p * LANES, (p + 1) * LANES)
                query = query_ref[rows, lanes]
                key = kv_ref[side, :size, lanes]
                value = kv_ref[side, :size, C + p * LANES : C + (p + 1) * LANES]
                old = top_ref[rows, lanes]
                outs, tops = [], []
                for half in range(2):
                    score = scores_of(query, key, half, bias)
                    highest = jnp.maximum(
                        jnp.max(score, axis=1, keepdims=True), old[:, half * HEAD : half * HEAD + 1]
                    )
                    outs.append(weighted(score, highest, value))
                    tops.append(jnp.broadcast_to(highest, (BLOCK, LANES)))
                top = by_half(tops[0], tops[1])
                fade = jnp.exp(old - top)
                value_ref[rows, lanes] = value_ref[rows, lanes] * fade + by_half(
                    outs[0][:, :LANES], outs[1][:, :LANES]
                )
                sum_ref[rows, lanes] = sum_ref[rows, lanes] * fade + by_half(
                    outs[0][:, LANES:], outs[1][:, LANES:]
                )
                top_ref[rows, lanes] = top

        span(count, attend)
        return carry

    lax.fori_loop(0, 2 * blocks, one_block, 0)
    attended = (value_ref[...] / sum_ref[...]).astype(bf16)
    middle = latent_ref[...] + dot(attended, w_out_ref[...])
    normed = layer_norm(middle).astype(bf16)
    hidden = w_up_ref.shape[1]
    part = 512
    total = middle
    for k in range(0, hidden, part):
        raised = jax.nn.gelu(dot(normed, w_up_ref[:, k : k + part]), approximate=True).astype(bf16)
        total = total + dot(raised, w_down_ref[k : k + part, :])
    out_ref[...] = total.astype(bf16)


def finish(tags, before_tag, after_tag, before, after, w_heads, query, value, top, total, latent, w_out, w_up, w_down):
    voxels = query.shape[0]
    row = lambda t: t.reshape(1, voxels)
    return pl.pallas_call(
        finish_kernel,
        out_shape=jax.ShapeDtypeStruct((voxels, C), bf16),
        in_specs=[SMEM] * 3 + [VMEM] * 14,
        out_specs=VMEM,
        scratch_shapes=[
            pltpu.VMEM((2, voxels, 2 * C), bf16),
            pltpu.VMEM((voxels, LANES), i32),
            pltpu.VMEM((2, 1, voxels), i32),
            pltpu.VMEM((voxels, C), f32),
            pltpu.VMEM((voxels, C), f32),
            pltpu.VMEM((voxels, C), f32),
        ],
        compiler_params=params(26),
        name="finish",
    )(
        tags, before_tag, after_tag, row(tags), row(before_tag), row(after_tag), before, after, w_heads,
        query, value, top, total, latent, w_out, w_up, w_down
    )


def local(features, w_embed, owner_device, voxel_slot, window_ids, w_heads, w_out, w_up, w_down):
    devices = lax.axis_size(AXES)
    patches = features.shape[0]
    voxels = window_ids.shape[0]
    capacity = max(2, 2 * patches // devices)
    buffer = dispatch(
        features, w_embed, owner_device.reshape(1, patches), voxel_slot.reshape(1, patches), devices, capacity
    )
    buffer, tags = lax.optimization_barrier((buffer, window_ids + 1))
    arrived = lax.all_to_all(buffer, AXES, split_axis=0, concat_axis=0, tiled=True)
    before_tag = passed_along(tags, 1)
    after_tag = passed_along(tags, -1)
    arrived, before_tag, after_tag = lax.optimization_barrier((arrived, before_tag, after_tag))
    latent, normed = gather(arrived, voxels)
    before = passed_along(normed, 1)
    after = passed_along(normed, -1)
    query, value, top, total = near(tags, normed, w_heads)
    return finish(
        tags, before_tag, after_tag, before, after, w_heads, query, value, top, total, latent, w_out, w_up, w_down
    )


def solution(mesh):
    rows = P(AXES, None)
    return jax.shard_map(
        local,
        mesh=mesh,
        in_specs=(rows, P(), rows, P(AXES), P(AXES), P(), P(), P(), P()),
        out_specs=rows,
        check_vma=False,
    )
```

time: 205 us -> 125 us (0.61)
  the two profiles are of different devices: /device:TPU:5 before, /device:TPU:3 now
where the time goes in v1:
time: 125 us; the launch traced here: 124 us
  waiting for transfers between devices  48.5 us (39%)
  Pallas kernels  36.7 us (29%)
  starting transfers between devices  26.8 us (21%)
  local copies, waits for them, and re-layouts  10.8 us (9%)
    ppermute x4, waiting for transfers between devices, passed_along(): return lax.ppermute(block, AXES, route)  45.3 us
    pallas_call x1, Pallas kernels, finish(): pl.pallas_call(finish_kernel, out_shape=jax.ShapeDtypeStruct((voxels, C),...  18 us
    ppermute x4, starting transfers between devices, passed_along(): return lax.ppermute(block, AXES, route)  15.6 us
    all_to_all x1, starting transfers between devices, local(): lax.all_to_all(buffer, AXES, split_axis=0, concat_axis=0, tiled=True)  11.2 us
    unnamed x18, local copies, waits for them, and re-layouts  10.8 us
    pallas_call x1, Pallas kernels, near(): pl.pallas_call(near_kernel, out_shape=(jax.ShapeDtypeStruct((voxels, C),...  7.21 us
    pallas_call x1, Pallas kernels, dispatch(): pl.pallas_call(dispatch_kernel, out_shape=jax.ShapeDtypeStruct((devices,...  6.19 us
    pallas_call x1, Pallas kernels, gather(): pl.pallas_call(gather_kernel, out_shape=(jax.ShapeDtypeStruct((voxels, C)...  5.35 us
  transfers between devices with their start and end apart: 5, of which 5 were waited for; matrix products, arithmetic and copies ran while one was open for 0% of the time, Pallas kernels for 6%

profile of v1, /device:TPU:3, one launch (start us, length us, event | category | flops | bytes accessed | tf_op | source)
XLA Modules:
  0.0 123.6 jit_solution(9270181000939638490)
XLA Ops:
  0.0 0.7 broadcast_add_fusion.tag_ref
  0.7 0.0 copy-start.4
  0.7 1.6 %copy-done.4 = bf16[1024,1024]{1,0:T(8,128)(2,1)S(1)} copy-done((bf16[1024,1024]{1,0:T(8,128)(2,1)S(1)}, bf16[1024,1024]{1,0:T(8,128)(2,1)}, u32[]{:S(2)}) %copy-start.4) | copy-done | bytes 2097176
  2.3 0.0 copy-start.5
  2.3 1.4 %copy-done.5 = bf16[1024,768]{1,0:T(8,128)(2,1)S(1)} copy-done((bf16[1024,768]{1,0:T(8,128)(2,1)S(1)}, bf16[1024,768]{1,0:T(8,128)(2,1)}, u32[]{:S(2)}) %copy-start.5) | copy-done | bytes 1572888
  3.7 0.0 copy-start.7
  3.7 0.7 copy-done.7
  4.4 0.0 copy-start.8
  4.4 0.7 copy-done.8
  5.1 6.2 %dispatch.1 = bf16[128,104,128]{2,1,0:T(8,128)(2,1)S(1)} custom-call(bf16[1024,1024]{1,0:T(8,128)(2,1)S(1)} %copy-done.4, bf16[1024,768]{1,0:T(8,128)(2,1)S(1)} %copy-done.5, s32[1,1024]{1,0:T(1,128)S(1)} %bitcast.9, s32[1,1024]{1,0:T(1,128)S(1)} %bitcast.10), custom_call_target="tpu_custom_call" | custom-call | tf_op jit(solution)/shard_map/dispatch/pallas_call | solution.py:105
  11.3 0.0 copy-start.1
  11.3 1.7 %copy-done.1 = bf16[128,104,128]{2,1,0:T(8,128)(2,1)} copy-done((bf16[128,104,128]{2,1,0:T(8,128)(2,1)}, bf16[128,104,128]{2,1,0:T(8,128)(2,1)S(1)}, u32[]{:S(2)}) %copy-start.1) | copy-done | bytes 3407896
  13.0 0.0 copy-start
  13.0 11.2 %all-to-all-start = ((bf16[128,104,128]{2,1,0:T(8,128)(2,1)}), bf16[128,104,128]{2,1,0:T(8,128)(2,1)}, u32[]{:S(2)}, u32[]{:S(2)}) async-start(bf16[128,104,128]{2,1,0:T(8,128)(2,1)} %copy-done.1), calls=%async_computation | async-start | bytes 6815744 | tf_op jit(solution)/shard_map/all_to_all | solution.py:397
  24.3 7.5 %collective-permute-start.1 = (s32[512]{0:T(512)S(1)}, s32[512]{0:T(512)S(1)}, u32[]{:S(2)}, u32[]{:S(2)}) collective-permute-start(s32[512]{0:T(512)S(1)} %broadcast_add_fusion.tag_ref), channel_id=1, source_target_pairs={{1,0},{2,1},{3,2},{4,3},{5,4},{6,5},{7,6},{8,7},{9,8},{10,9},{11,1... | collective-permute-start | bytes 6152 | tf_op jit(solution)/shard_map/ppermute | solution.py:26
  31.8 1.9 %collective-permute-start = (s32[512]{0:T(512)S(1)}, s32[512]{0:T(512)S(1)}, u32[]{:S(2)}, u32[]{:S(2)}) collective-permute-start(s32[512]{0:T(512)S(1)} %broadcast_add_fusion.tag_ref), channel_id=1, source_target_pairs={{0,1},{1,2},{2,3},{3,4},{4,5},{5,6},{6,7},{7,8},{8,9},{9,10},{10,1... | collective-permute-start | bytes 6152 | tf_op jit(solution)/shard_map/ppermute | solution.py:26
  33.7 25.3 %collective-permute-done.1.after_tag_ref = s32[512]{0:T(512)S(1)} collective-permute-done((s32[512]{0:T(512)S(1)}, s32[512]{0:T(512)S(1)}, u32[]{:S(2)}, u32[]{:S(2)}) %collective-permute-start.1) | collective-permute-done | bytes 2080 | tf_op jit(solution)/shard_map/ppermute | solution.py:26
  59.1 4.1 %collective-permute-done.before_tag_ref = s32[512]{0:T(512)S(1)} collective-permute-done((s32[512]{0:T(512)S(1)}, s32[512]{0:T(512)S(1)}, u32[]{:S(2)}, u32[]{:S(2)}) %collective-permute-start) | collective-permute-done | bytes 2080 | tf_op jit(solution)/shard_map/ppermute | solution.py:26
  63.2 3.1 %all-to-all-done.arrived_ref = bf16[128,104,128]{2,1,0:T(8,128)(2,1)} async-done(((bf16[128,104,128]{2,1,0:T(8,128)(2,1)}), bf16[128,104,128]{2,1,0:T(8,128)(2,1)}, u32[]{:S(2)}, u32[]{:S(2)}) %all-to-all-start) | async-done | bytes 3407904 | tf_op jit(solution)/shard_map/all_to_all | solution.py:397
  66.3 5.3 %gather.1 = (f32[512,768]{1,0:T(8,128)S(1)}, bf16[512,768]{1,0:T(8,128)(2,1)S(1)}) custom-call(bf16[128,104,128]{2,1,0:T(8,128)(2,1)} %all-to-all-done.arrived_ref), custom_call_target="tpu_custom_call" | custom-call | tf_op jit(solution)/shard_map/gather/pallas_call | solution.py:172
  71.7 4.2 %collective-permute-start.3 = (bf16[512,768]{1,0:T(8,128)(2,1)S(1)}, bf16[512,768]{1,0:T(8,128)(2,1)S(1)}, u32[]{:S(2)}, u32[]{:S(2)}) collective-permute-start(bf16[512,768]{1,0:T(8,128)(2,1)S(1)} %get-tuple-element.21.normed_ref), channel_id=1, source_target_pairs={{1,0},{2,1},{3,2},{4,3},{5,4},{6,5},{7,6},{8,7},{9,8},{10,9},{11,1... | collective-permute-start | bytes 2359304 | tf_op jit(solution)/shard_map/ppermute | solution.py:26
  75.9 1.9 %collective-permute-start.2 = (bf16[512,768]{1,0:T(8,128)(2,1)S(1)}, bf16[512,768]{1,0:T(8,128)(2,1)S(1)}, u32[]{:S(2)}, u32[]{:S(2)}) collective-permute-start(bf16[512,768]{1,0:T(8,128)(2,1)S(1)} %get-tuple-element.21.normed_ref), channel_id=1, source_target_pairs={{0,1},{1,2},{2,3},{3,4},{4,5},{5,6},{6,7},{7,8},{8,9},{9,10},{10,1... | collective-permute-start | bytes 2359304 | tf_op jit(solution)/shard_map/ppermute | solution.py:26
  77.9 0.0 copy-done
  77.9 0.0 copy-start.6
  77.9 7.2 %near.1 = (bf16[512,768]{1,0:T(8,128)(2,1)S(1)}, f32[512,768]{1,0:T(8,128)S(1)}, f32[512,768]{1,0:T(8,128)S(1)}, f32[512,768]{1,0:T(8,128)S(1)}) custom-call(s32[512]{0:T(512)S(1)} %broadcast_add_fusion.tag_ref, s32[1,512]{1,0:T(1,128)S(1)} %bitcast.5, bf16[512,768]{1,0:T(8,128)(2,1)S(1)} %get-tuple-element.21.normed_ref, bf16[768,2304]{1,0:T(8,128)(2,1)S(1)} %copy-done), custom_call_target="tpu_custom_call" | custom-call | tf_op jit(solution)/shard_map/near/pallas_call | solution.py:265
  85.1 8.2 %collective-permute-done.3.after_ref = bf16[512,768]{1,0:T(8,128)(2,1)S(1)} collective-permute-done((bf16[512,768]{1,0:T(8,128)(2,1)S(1)}, bf16[512,768]{1,0:T(8,128)(2,1)S(1)}, u32[]{:S(2)}, u32[]{:S(2)}) %collective-permute-start.3) | collective-permute-done | bytes 786464 | tf_op jit(solution)/shard_map/ppermute | solution.py:26
  93.3 7.7 %collective-permute-done.2.before_ref = bf16[512,768]{1,0:T(8,128)(2,1)S(1)} collective-permute-done((bf16[512,768]{1,0:T(8,128)(2,1)S(1)}, bf16[512,768]{1,0:T(8,128)(2,1)S(1)}, u32[]{:S(2)}, u32[]{:S(2)}) %collective-permute-start.2) | collective-permute-done | bytes 786464 | tf_op jit(solution)/shard_map/ppermute | solution.py:26
  101.0 0.0 copy-done.6
  101.0 0.0 copy-start.2
  101.0 2.3 %copy-done.2 = bf16[768,3072]{1,0:T(8,128)(2,1)S(1)} copy-done((bf16[768,3072]{1,0:T(8,128)(2,1)S(1)}, bf16[768,3072]{1,0:T(8,128)(2,1)}, u32[]{:S(2)}) %copy-start.2) | copy-done | bytes 4718616
  103.3 0.0 copy-start.3
  103.3 2.3 %copy-done.3 = bf16[3072,768]{1,0:T(8,128)(2,1)S(1)} copy-done((bf16[3072,768]{1,0:T(8,128)(2,1)S(1)}, bf16[3072,768]{1,0:T(8,128)(2,1)}, u32[]{:S(2)}) %copy-start.3) | copy-done | bytes 4718616
  105.7 18.0 %finish.1 = bf16[512,768]{1,0:T(8,128)(2,1)} custom-call(s32[512]{0:T(512)S(1)} %broadcast_add_fusion.tag_ref, s32[512]{0:T(512)S(1)} %collective-permute-done.before_tag_ref, s32[512]{0:T(512)S(1)} %collective-permute-done.1.after_tag_ref, s32[1,512]{1,0:T(1,128)S(1)} %bitcast.6, s32[1,512]{1,0:T(1,128)S(1)} %bitcast.8, s32[1,512]{1,0:T(1,128)S(1)} %bitcast.7, ...), custom_call_target="tpu_custom_call" | custom-call | tf_op jit(solution)/shard_map/finish/pallas_call | solution.py:367
Async XLA Ops:
  0.7 1.6 %copy-start.4 = (bf16[1024,1024]{1,0:T(8,128)(2,1)S(1)}, bf16[1024,1024]{1,0:T(8,128)(2,1)}, u32[]{:S(2)}) copy-start(bf16[1024,1024]{1,0:T(8,128)(2,1)} %features_ref.1) | copy-start | bytes 6291460
  2.3 1.4 %copy-start.5 = (bf16[1024,768]{1,0:T(8,128)(2,1)S(1)}, bf16[1024,768]{1,0:T(8,128)(2,1)}, u32[]{:S(2)}) copy-start(bf16[1024,768]{1,0:T(8,128)(2,1)} %embed_ref.1) | copy-start | bytes 4718596
  3.7 0.7 copy-start.7
  4.4 0.7 copy-start.8
  11.3 1.8 %copy-start.1 = (bf16[128,104,128]{2,1,0:T(8,128)(2,1)}, bf16[128,104,128]{2,1,0:T(8,128)(2,1)S(1)}, u32[]{:S(2)}) copy-start(bf16[128,104,128]{2,1,0:T(8,128)(2,1)S(1)} %dispatch.1) | copy-start | bytes 10223620
  13.0 64.9 %copy-start = (bf16[768,2304]{1,0:T(8,128)(2,1)S(1)}, bf16[768,2304]{1,0:T(8,128)(2,1)}, u32[]{:S(2)}) copy-start(bf16[768,2304]{1,0:T(8,128)(2,1)} %heads_ref.3) | copy-start | bytes 10616836
  13.0 53.3 %all-to-all-start = ((bf16[128,104,128]{2,1,0:T(8,128)(2,1)}), bf16[128,104,128]{2,1,0:T(8,128)(2,1)}, u32[]{:S(2)}, u32[]{:S(2)}) async-start(bf16[128,104,128]{2,1,0:T(8,128)(2,1)} %copy-done.1), calls=%async_computation | async-start | bytes 6815744 | tf_op jit(solution)/shard_map/all_to_all | solution.py:397
  24.3 34.8 %collective-permute-start.1 = (s32[512]{0:T(512)S(1)}, s32[512]{0:T(512)S(1)}, u32[]{:S(2)}, u32[]{:S(2)}) collective-permute-start(s32[512]{0:T(512)S(1)} %broadcast_add_fusion.tag_ref), channel_id=1, source_target_pairs={{1,0},{2,1},{3,2},{4,3},{5,4},{6,5},{7,6},{8,7},{9,8},{10,9},{11,1... | collective-permute-start | bytes 6152 | tf_op jit(solution)/shard_map/ppermute | solution.py:26
  31.8 31.4 %collective-permute-start = (s32[512]{0:T(512)S(1)}, s32[512]{0:T(512)S(1)}, u32[]{:S(2)}, u32[]{:S(2)}) collective-permute-start(s32[512]{0:T(512)S(1)} %broadcast_add_fusion.tag_ref), channel_id=1, source_target_pairs={{0,1},{1,2},{2,3},{3,4},{4,5},{5,6},{6,7},{7,8},{8,9},{9,10},{10,1... | collective-permute-start | bytes 6152 | tf_op jit(solution)/shard_map/ppermute | solution.py:26
  71.7 21.6 %collective-permute-start.3 = (bf16[512,768]{1,0:T(8,128)(2,1)S(1)}, bf16[512,768]{1,0:T(8,128)(2,1)S(1)}, u32[]{:S(2)}, u32[]{:S(2)}) collective-permute-start(bf16[512,768]{1,0:T(8,128)(2,1)S(1)} %get-tuple-element.21.normed_ref), channel_id=1, source_target_pairs={{1,0},{2,1},{3,2},{4,3},{5,4},{6,5},{7,6},{8,7},{9,8},{10,9},{11,1... | collective-permute-start | bytes 2359304 | tf_op jit(solution)/shard_map/ppermute | solution.py:26
  75.9 25.1 %collective-permute-start.2 = (bf16[512,768]{1,0:T(8,128)(2,1)S(1)}, bf16[512,768]{1,0:T(8,128)(2,1)S(1)}, u32[]{:S(2)}, u32[]{:S(2)}) collective-permute-start(bf16[512,768]{1,0:T(8,128)(2,1)S(1)} %get-tuple-element.21.normed_ref), channel_id=1, source_target_pairs={{0,1},{1,2},{2,3},{3,4},{4,5},{5,6},{6,7},{7,8},{8,9},{9,10},{10,1... | collective-permute-start | bytes 2359304 | tf_op jit(solution)/shard_map/ppermute | solution.py:26
  77.9 23.1 %copy-start.6 = (bf16[768,768]{1,0:T(8,128)(2,1)S(1)}, bf16[768,768]{1,0:T(8,128)(2,1)}, u32[]{:S(2)}) copy-start(bf16[768,768]{1,0:T(8,128)(2,1)} %w_out_ref.1) | copy-start | bytes 3538948
  101.0 2.3 %copy-start.2 = (bf16[768,3072]{1,0:T(8,128)(2,1)S(1)}, bf16[768,3072]{1,0:T(8,128)(2,1)}, u32[]{:S(2)}) copy-start(bf16[768,3072]{1,0:T(8,128)(2,1)} %w_up_ref.1) | copy-start | bytes 14155780
  103.3 2.3 %copy-start.3 = (bf16[3072,768]{1,0:T(8,128)(2,1)S(1)}, bf16[3072,768]{1,0:T(8,128)(2,1)}, u32[]{:S(2)}) copy-start(bf16[3072,768]{1,0:T(8,128)(2,1)} %w_down_ref.1) | copy-start | bytes 14155780

commit v2 on v1

v2 whole, which is shorter than its diff:
```python
import jax
import jax.numpy as jnp
from jax import lax
from jax.experimental import pallas as pl
from jax.experimental.pallas import tpu as pltpu
from jax.sharding import PartitionSpec as P

C = 768
HEADS = 12
HEAD = C // HEADS
PAIRS = HEADS // 2
LANES = 128
CHUNKS = C // LANES
BLOCK = 128
epsilon = 1e-06
AXES = ("view", "vox")
f32 = jnp.float32
bf16 = jnp.bfloat16
i32 = jnp.int32
MASKED = -1e30


def passed_along(block, distance):
    devices = range(lax.axis_size(AXES))
    route = [(i - distance, i) for i in devices if i - distance in devices]
    return lax.ppermute(block, AXES, route)


def layer_norm(values):
    average = jnp.mean(values, axis=-1, keepdims=True)
    centered = values - average
    variance = jnp.mean(centered * centered, axis=-1, keepdims=True)
    return centered * lax.rsqrt(variance + epsilon)


def across(a, b):
    return lax.dot_general(a, b, (((1,), (1,)), ((), ())), preferred_element_type=f32)


def dot(a, b):
    return jnp.dot(a, b, preferred_element_type=f32)


def iota(shape, dim):
    return lax.broadcasted_iota(i32, shape, dim)


def params(mib):
    return pltpu.CompilerParams(vmem_limit_bytes=mib << 20)


GROUPS = 4


def dispatch_kernel(
    features_hbm, embed_hbm, owner_hbm, slot_hbm, out_hbm,
    features_ref, embed_ref, owner_ref, slot_ref, out_ref, payload_ref, position_ref, digits_ref, in_sem, out_sem
):
    copies = [
        pltpu.make_async_copy(source, target, in_sem.at[k])
        for k, (source, target) in enumerate(
            (
                (owner_hbm, owner_ref),
                (slot_hbm, slot_ref),
                (features_hbm, features_ref),
                (embed_hbm, embed_ref),
            )
        )
    ]
    for copy in copies:
        copy.start()
    patches = features_ref.shape[0]
    devices = digits_ref.shape[1]
    group = devices // GROUPS
    capacity = (out_ref.shape[1] - 8) // CHUNKS
    part = 256
    mine = lax.rem(lax.axis_index("vox"), LANES // capacity)
    earlier = jnp.where(iota((part, part), 0) < iota((part, part), 1), 1.0, 0.0).astype(bf16)
    copies[0].wait()
    copies[1].wait()
    owner = owner_ref[...]
    hits = jnp.where(iota((devices, patches), 0) == owner, 1.0, 0.0)
    running = jnp.zeros((devices, 1), f32)
    ranks = []
    for start in range(0, patches, part):
        here = hits[:, start : start + part]
        before = dot(here.astype(bf16), earlier) + running
        running = running + jnp.sum(here, axis=1, keepdims=True)
        ranks.append(jnp.sum(here * before, axis=0, keepdims=True))
    rank = jnp.concatenate(ranks, axis=1).astype(i32)
    position_ref[...] = owner * capacity + rank
    place = jnp.where(iota((LANES, patches), 0) == rank + capacity * mine, 1.0, 0.0).astype(bf16)
    code = slot_ref[...] + 1
    digits_ref[0] = across((hits * (code >> 4).astype(f32)).astype(bf16), place)
    digits_ref[1] = across((hits * (code & 15).astype(f32)).astype(bf16), place)
    copies[2].wait()
    copies[3].wait()
    payload_ref[...] = dot(features_ref[...], embed_ref[...]).astype(bf16)
    rows = group * capacity
    sends = []
    for g in range(GROUPS):
        here = slice(g * group, (g + 1) * group)
        chosen = jnp.where(iota((rows, patches), 0) + g * rows == position_ref[...], 1.0, 0.0)
        block = dot(chosen.astype(bf16), payload_ref[...]).astype(bf16)
        for c in range(CHUNKS):
            out_ref[here, c * capacity : (c + 1) * capacity, :] = block[
                :, c * LANES : (c + 1) * LANES
            ].reshape(group, capacity, LANES)
        high = jnp.broadcast_to(digits_ref[0, here, :][:, None, :], (group, 8, LANES))
        low = jnp.broadcast_to(digits_ref[1, here, :][:, None, :], (group, 8, LANES))
        out_ref[here, CHUNKS * capacity :, :] = jnp.where(
            iota((group, 8, LANES), 1) < 4, high, low
        ).astype(bf16)
        send = pltpu.make_async_copy(out_ref.at[here], out_hbm.at[here], out_sem.at[g])
        send.start()
        sends.append(send)
    for send in sends:
        send.wait()


def kept(*arrays):
    return [pltpu.with_memory_space_constraint(array, pltpu.HBM) for array in arrays]


HBM = pl.BlockSpec(memory_space=pltpu.HBM)
VMEM = pl.BlockSpec(memory_space=pltpu.VMEM)
SMEM = pl.BlockSpec(memory_space=pltpu.SMEM)


def dispatch(features, w_embed, owner, slot, devices, capacity):
    patches, width = features.shape
    tall = CHUNKS * capacity + 8
    return pl.pallas_call(
        dispatch_kernel,
        out_shape=pltpu.HBM((devices, tall, LANES), bf16),
        in_specs=[HBM] * 4,
        out_specs=HBM,
        scratch_shapes=[
            pltpu.VMEM((patches, width), bf16),
            pltpu.VMEM((width, C), bf16),
            pltpu.VMEM((1, patches), i32),
            pltpu.VMEM((1, patches), i32),
            pltpu.VMEM((devices, tall, LANES), bf16),
            pltpu.VMEM((patches, C), bf16),
            pltpu.VMEM((1, patches), i32),
            pltpu.VMEM((2, devices, LANES), f32),
            pltpu.SemaphoreType.DMA((4,)),
            pltpu.SemaphoreType.DMA((GROUPS,)),
        ],
        compiler_params=params(32),
        name="dispatch",
    )(*kept(features, w_embed, owner, slot))


def gather_kernel(arrived_hbm, latent_ref, normed_ref, arrived_ref, digit_ref, member_ref, sem):
    sources = arrived_ref.shape[0]
    capacity = arrived_ref.shape[1] // CHUNKS
    tall = CHUNKS * capacity
    voxels = latent_ref.shape[0]
    each = LANES // capacity
    digit_copy = pltpu.make_async_copy(arrived_hbm.at[:, tall:, :], digit_ref, sem.at[0])
    digit_copy.start()
    data_copy = pltpu.make_async_copy(arrived_hbm.at[:, :tall, :], arrived_ref, sem.at[1])
    data_copy.start()
    digit_copy.wait()
    digits = jnp.sum(digit_ref[...].astype(f32).reshape(sources // each, each, 8, LANES), axis=1)
    code = (digits[:, 0, :] * 16.0 + digits[:, 4, :]).astype(i32) - 1
    counted = jnp.zeros((voxels, LANES), f32)
    for g in range(sources // each):
        member = jnp.where(iota((voxels, LANES), 0) == code[g : g + 1], 1.0, 0.0)
        counted = counted + member
        member_ref[:, g * LANES : (g + 1) * LANES] = member.astype(bf16)
    counts = jnp.sum(counted, axis=1, keepdims=True)
    data_copy.wait()
    data = jnp.concatenate(
        [
            arrived_ref[:, c * capacity : (c + 1) * capacity, :].reshape(sources * capacity, LANES)
            for c in range(CHUNKS)
        ],
        axis=1,
    )
    latent = dot(member_ref[...], data) / jnp.maximum(counts, 1.0)
    latent_ref[...] = latent
    normed_ref[...] = layer_norm(latent).astype(bf16)


def gather(arrived, voxels):
    sources, tall, _ = arrived.shape
    return pl.pallas_call(
        gather_kernel,
        out_shape=(
            jax.ShapeDtypeStruct((voxels, C), f32),
            jax.ShapeDtypeStruct((voxels, C), bf16),
        ),
        in_specs=[HBM],
        out_specs=(VMEM, VMEM),
        scratch_shapes=[
            pltpu.VMEM((sources, tall - 8, LANES), bf16),
            pltpu.VMEM((sources, 8, LANES), bf16),
            pltpu.VMEM((voxels, sources * ((tall - 8) // CHUNKS)), bf16),
            pltpu.SemaphoreType.DMA((2,)),
        ],
        compiler_params=params(24),
        name="gather",
    )(arrived)


def column_of(row):
    return jnp.broadcast_to(row, (LANES, row.shape[1])).T


def by_half(both):
    first, second = both[:BLOCK], both[BLOCK:]
    return jnp.where(iota(first.shape, 1) < HEAD, first, second)


def scores_of(query_pair, key_pair, bias):
    left = iota(query_pair.shape, 1) < HEAD
    none = jnp.zeros_like(query_pair)
    both = jnp.concatenate([jnp.where(left, query_pair, none), jnp.where(left, none, query_pair)], axis=0)
    return across(both, key_pair) + bias


def weighted(score, highest, value_pair):
    exponent = jnp.exp(score - highest).astype(bf16)
    wide = jnp.concatenate([value_pair, jnp.ones_like(value_pair)], axis=1)
    return dot(exponent, wide)


def bias_of(column, row):
    tiles = [
        jnp.where(column == row[:, k : k + LANES], 0.0, MASKED) for k in range(0, row.shape[1], LANES)
    ]
    bias = jnp.concatenate(tiles, axis=1)
    return jnp.concatenate([bias, bias], axis=0)


def rims(tag_ref, before_tag_ref, after_tag_ref):
    voxels = tag_ref.shape[0]
    blocks = voxels // BLOCK
    start_tag, end_tag = tag_ref[0], tag_ref[voxels - 1]
    head = i32(0)
    tail = i32(0)
    for k in range(blocks):
        head += (tag_ref[k * BLOCK] == start_tag).astype(i32)
        tail += (tag_ref[k * BLOCK + BLOCK - 1] == end_tag).astype(i32)
    ring = [lax.axis_index(axis) for axis in AXES]
    ends = [lax.axis_size(axis) - 1 for axis in AXES]
    first = jnp.logical_and(ring[0] == 0, ring[1] == 0)
    final = jnp.logical_and(ring[0] == ends[0], ring[1] == ends[1])
    head = jnp.where(jnp.logical_or(first, before_tag_ref[voxels - 1] != start_tag), 0, head)
    tail = jnp.where(jnp.logical_or(final, after_tag_ref[0] != end_tag), 0, tail)
    return head, tail


SPAN = 2 * BLOCK


def feed_forward(attended, latent, w_out_ref, w_up_ref, w_down_ref):
    middle = latent + dot(attended, w_out_ref[...])
    normed = layer_norm(middle).astype(bf16)
    total = middle
    part = 512
    for k in range(0, w_up_ref.shape[1], part):
        raised = jax.nn.gelu(dot(normed, w_up_ref[:, k : k + part]), approximate=True).astype(bf16)
        total = total + dot(raised, w_down_ref[k : k + part, :])
    return total.astype(bf16)


def near_kernel(
    tag_ref, before_tag_ref, after_tag_ref, tag_row_ref, normed_ref, heads_ref, latent_ref, w_out_ref, up_hbm, down_hbm,
    query_ref, value_ref, top_ref, sum_ref, out_ref, kv_ref, column_ref, up_ref, down_ref, sem
):
    up_copy = pltpu.make_async_copy(up_hbm, up_ref, sem.at[0])
    down_copy = pltpu.make_async_copy(down_hbm, down_ref, sem.at[1])
    up_copy.start()
    down_copy.start()
    voxels = normed_ref.shape[0]
    blocks = voxels // BLOCK
    normed = normed_ref[...]
    query_ref[...] = dot(normed, heads_ref[:, :C]).astype(bf16) * jnp.asarray(HEAD**-0.5, bf16)
    kv_ref[...] = dot(normed, heads_ref[:, C:]).astype(bf16)
    column_ref[...] = column_of(tag_row_ref[...])

    def one_block(b, carry):
        rows = pl.ds(pl.multiple_of(b * BLOCK, BLOCK), BLOCK)
        first, last = tag_ref[b * BLOCK], tag_ref[b * BLOCK + BLOCK - 1]
        low = i32(0)
        high = i32(0)
        for k in range(blocks):
            low = low + (tag_ref[k * BLOCK + BLOCK - 1] < first).astype(i32)
            high = high + (tag_ref[k * BLOCK] <= last).astype(i32)
        count = high - low

        def attend(n):
            keys = pl.ds(pl.multiple_of(low * BLOCK, BLOCK), n * BLOCK)
            bias = bias_of(column_ref[rows, :], tag_row_ref[:, keys])
            for p in range(PAIRS):
                lanes = slice(p * LANES, (p + 1) * LANES)
                score = scores_of(query_ref[rows, lanes], kv_ref[keys, lanes], bias)
                highest = jnp.max(score, axis=1, keepdims=True)
                result = weighted(score, highest, kv_ref[keys, C + p * LANES : C + (p + 1) * LANES])
                value_ref[rows, lanes] = by_half(result[:, :LANES])
                sum_ref[rows, lanes] = by_half(result[:, LANES:])
                top_ref[rows, lanes] = by_half(jnp.broadcast_to(highest, (2 * BLOCK, LANES)))

        for n in range(1, blocks + 1):
            pl.when(count == n)(lambda n=n: attend(n))
        return carry

    lax.fori_loop(0, blocks, one_block, 0)
    head, tail = rims(tag_ref, before_tag_ref, after_tag_ref)
    up_copy.wait()
    down_copy.wait()

    def one_span(k, carry):
        start = jnp.minimum((head + 2 * k) * BLOCK, voxels - SPAN)
        rows = pl.ds(pl.multiple_of(start, BLOCK), SPAN)
        attended = (value_ref[rows, :] / sum_ref[rows, :]).astype(bf16)
        out_ref[rows, :] = feed_forward(attended, latent_ref[rows, :], w_out_ref, up_ref, down_ref)
        return carry

    lax.fori_loop(0, (jnp.maximum(blocks - head - tail, 0) + 1) // 2, one_span, 0)


def near(tags, before_tag, after_tag, normed, w_heads, latent, w_out, w_up, w_down):
    voxels = normed.shape[0]
    state = jax.ShapeDtypeStruct((voxels, C), f32)
    rows = jax.ShapeDtypeStruct((voxels, C), bf16)
    return pl.pallas_call(
        near_kernel,
        out_shape=(rows, state, state, state, rows),
        in_specs=[SMEM] * 3 + [VMEM] * 5 + [HBM] * 2,
        out_specs=(VMEM,) * 5,
        scratch_shapes=[
            pltpu.VMEM((voxels, 2 * C), bf16),
            pltpu.VMEM((voxels, LANES), i32),
            pltpu.VMEM(w_up.shape, bf16),
            pltpu.VMEM(w_down.shape, bf16),
            pltpu.SemaphoreType.DMA((2,)),
        ],
        compiler_params=params(32),
        name="near",
    )(tags, before_tag, after_tag, tags.reshape(1, voxels), normed, w_heads, latent, w_out, *kept(w_up, w_down))


def finish_kernel(
    tag_ref, before_tag_ref, after_tag_ref, tag_row_ref, before_row_ref, after_row_ref,
    before_ref, after_ref, heads_ref, query_ref, value_ref, top_ref, sum_ref, near_out_ref, latent_ref,
    w_out_ref, up_hbm, down_hbm, out_ref,
    kv_ref, column_ref, row_ref, late_value_ref, late_sum_ref, late_top_ref, late_latent_ref, late_out_ref,
    up_ref, down_ref, sem
):
    up_copy = pltpu.make_async_copy(up_hbm, up_ref, sem.at[0])
    down_copy = pltpu.make_async_copy(down_hbm, down_ref, sem.at[1])
    up_copy.start()
    down_copy.start()
    voxels = query_ref.shape[0]
    blocks = voxels // BLOCK
    sizes = (2, blocks)
    column_ref[...] = column_of(tag_row_ref[...])
    start_tag, end_tag = tag_ref[0], tag_ref[voxels - 1]
    head, tail = rims(tag_ref, before_tag_ref, after_tag_ref)
    late = jnp.minimum(head + tail, blocks)
    before_count = i32(0)
    after_count = i32(0)
    for k in range(blocks):
        before_count += (before_tag_ref[k * BLOCK + BLOCK - 1] == start_tag).astype(i32)
        after_count += (after_tag_ref[k * BLOCK] == end_tag).astype(i32)
    before_count = jnp.where(head > 0, before_count, 0)
    after_count = jnp.where(tail > 0, after_count, 0)

    def project(side, source_ref, source_row_ref, n):
        size = n * BLOCK
        start = 0 if side else voxels - size
        kv_ref[side, :size] = dot(source_ref[start : start + size, :], heads_ref[:, C:]).astype(bf16)
        row_ref[side, :, :size] = source_row_ref[:, start : start + size]

    def span(count, action):
        for lower, n in zip((0,) + sizes, sizes):
            pl.when(jnp.logical_and(count > lower, count <= n))(lambda n=n: action(n))

    span(before_count, lambda n: project(0, before_ref, before_row_ref, n))
    span(after_count, lambda n: project(1, after_ref, after_row_ref, n))
    out_ref[...] = near_out_ref[...]

    def rows_of(k):
        b = jnp.where(k < head, k, k + blocks - late)
        return b, pl.ds(pl.multiple_of(b * BLOCK, BLOCK), BLOCK)

    def one_late(k, carry):
        b, rows = rows_of(k)
        put = pl.ds(pl.multiple_of(k * BLOCK, BLOCK), BLOCK)
        late_value_ref[put, :] = value_ref[rows, :]
        late_sum_ref[put, :] = sum_ref[rows, :]
        late_top_ref[put, :] = top_ref[rows, :]
        late_latent_ref[put, :] = latent_ref[rows, :]

        def one_side(side, carry):
            touched = jnp.where(side == 0, b < head, b >= blocks - tail)
            count = jnp.where(touched, jnp.where(side == 0, before_count, after_count), 0)

            def attend(n):
                size = n * BLOCK
                bias = bias_of(column_ref[rows, :], row_ref[side, :, :size])
                for p in range(PAIRS):
                    lanes = slice(p * LANES, (p + 1) * LANES)
                    old = late_top_ref[put, lanes]
                    score = scores_of(query_ref[rows, lanes], kv_ref[side, :size, lanes], bias)
                    known = jnp.concatenate([old[:, :1], old[:, HEAD : HEAD + 1]], axis=0)
                    highest = jnp.maximum(jnp.max(score, axis=1, keepdims=True), known)
                    result = weighted(score, highest, kv_ref[side, :size, C + p * LANES : C + (p + 1) * LANES])
                    top = by_half(jnp.broadcast_to(highest, (2 * BLOCK, LANES)))
                    fade = jnp.exp(old - top)
                    late_value_ref[put, lanes] = late_value_ref[put, lanes] * fade + by_half(result[:, :LANES])
                    late_sum_ref[put, lanes] = late_sum_ref[put, lanes] * fade + by_half(result[:, LANES:])
                    late_top_ref[put, lanes] = top

            span(count, attend)
            return carry

        return lax.fori_loop(0, 2, one_side, carry)

    lax.fori_loop(0, late, one_late, 0)
    up_copy.wait()
    down_copy.wait()

    def one_span(k, carry):
        rows = pl.ds(pl.multiple_of(k * SPAN, SPAN), SPAN)
        attended = (late_value_ref[rows, :] / late_sum_ref[rows, :]).astype(bf16)
        late_out_ref[rows, :] = feed_forward(attended, late_latent_ref[rows, :], w_out_ref, up_ref, down_ref)
        return carry

    lax.fori_loop(0, (late + 1) // 2, one_span, 0)

    def put_back(k, carry):
        _, rows = rows_of(k)
        out_ref[rows, :] = late_out_ref[pl.ds(pl.multiple_of(k * BLOCK, BLOCK), BLOCK), :]
        return carry

    lax.fori_loop(0, late, put_back, 0)


def finish(
    tags, before_tag, after_tag, before, after, w_heads, query, value, top, total, near_out, latent, w_out, w_up, w_down
):
    voxels = query.shape[0]
    row = lambda t: t.reshape(1, voxels)
    state = pltpu.VMEM((voxels, C), f32)
    return pl.pallas_call(
        finish_kernel,
        out_shape=jax.ShapeDtypeStruct((voxels, C), bf16),
        in_specs=[SMEM] * 3 + [VMEM] * 13 + [HBM] * 2,
        out_specs=VMEM,
        scratch_shapes=[
            pltpu.VMEM((2, voxels, 2 * C), bf16),
            pltpu.VMEM((voxels, LANES), i32),
            pltpu.VMEM((2, 1, voxels), i32),
            state,
            state,
            state,
            state,
            pltpu.VMEM((voxels, C), bf16),
            pltpu.VMEM(w_up.shape, bf16),
            pltpu.VMEM(w_down.shape, bf16),
            pltpu.SemaphoreType.DMA((2,)),
        ],
        compiler_params=params(36),
        name="finish",
    )(
        tags, before_tag, after_tag, row(tags), row(before_tag), row(after_tag), before, after, w_heads,
        query, value, top, total, near_out, latent, w_out, *kept(w_up, w_down)
    )


def local(features, w_embed, owner_device, voxel_slot, window_ids, w_heads, w_out, w_up, w_down):
    devices = lax.axis_size(AXES)
    patches = features.shape[0]
    voxels = window_ids.shape[0]
    capacity = max(2, 2 * patches // devices)
    buffer = dispatch(
        features, w_embed, owner_device.reshape(1, patches), voxel_slot.reshape(1, patches), devices, capacity
    )
    buffer, tags = lax.optimization_barrier((buffer, window_ids))
    arrived = lax.all_to_all(buffer, AXES, split_axis=0, concat_axis=0, tiled=True)
    before_tag = passed_along(tags, 1)
    after_tag = passed_along(tags, -1)
    arrived, before_tag, after_tag = lax.optimization_barrier((arrived, before_tag, after_tag))
    latent, normed = gather(arrived, voxels)
    before = passed_along(normed, 1)
    after = passed_along(normed, -1)
    query, value, top, total, out = near(
        tags, before_tag, after_tag, normed, w_heads, latent, w_out, w_up, w_down
    )
    return finish(
        tags, before_tag, after_tag, before, after, w_heads, query, value, top, total, out, latent, w_out, w_up, w_down
    )


def solution(mesh):
    rows = P(AXES, None)
    return jax.shard_map(
        local,
        mesh=mesh,
        in_specs=(rows, P(), rows, P(AXES), P(AXES), P(), P(), P(), P()),
        out_specs=rows,
        check_vma=False,
    )
```

time: 125 us -> 113 us (0.904)
  the two profiles are of different devices: /device:TPU:3 before, /device:TPU:5 now
where the time goes in v2:
time: 113 us; the launch traced here: 111 us
  waiting for transfers between devices  42.8 us (38%)
  Pallas kernels  40.8 us (36%)
  starting transfers between devices  27.6 us (24%)
    ppermute x4, waiting for transfers between devices, passed_along(): return lax.ppermute(block, AXES, route)  42.6 us
    pallas_call x1, Pallas kernels, finish(): pl.pallas_call(finish_kernel, out_shape=jax.ShapeDtypeStruct((voxels, C),...  16.7 us
    ppermute x4, starting transfers between devices, passed_along(): return lax.ppermute(block, AXES, route)  16.3 us
    pallas_call x1, Pallas kernels, near(): pl.pallas_call(near_kernel, out_shape=(rows, state, state, state, rows),...  11.7 us
    all_to_all x1, starting transfers between devices, local(): lax.all_to_all(buffer, AXES, split_axis=0, concat_axis=0, tiled=True)  11.2 us
    pallas_call x1, Pallas kernels, dispatch(): pl.pallas_call(dispatch_kernel, out_shape=pltpu.HBM((devices, tall, LANES...  8.23 us
    pallas_call x1, Pallas kernels, gather(): pl.pallas_call(gather_kernel, out_shape=(jax.ShapeDtypeStruct((voxels, C)...  4.22 us
  transfers between devices with their start and end apart: 5, of which 5 were waited for; matrix products, arithmetic and copies ran while one was open for 0% of the time, Pallas kernels for 10%

profile of v2, /device:TPU:5, one launch (start us, length us, event | category | flops | bytes accessed | tf_op | source)
XLA Modules:
  0.0 111.4 jit_solution(328215793497699299)
XLA Ops:
  0.0 8.2 %dispatch.1 = bf16[128,104,128]{2,1,0:T(8,128)(2,1)} custom-call(bf16[1024,1024]{1,0:T(8,128)(2,1)} %features_hbm.1, bf16[1024,768]{1,0:T(8,128)(2,1)} %embed_hbm.1, s32[1,1024]{1,0:T(1,128)} %bitcast.9, s32[1,1024]{1,0:T(1,128)} %bitcast.10), custom_call_target="tpu_custom_call" | custom-call | tf_op jit(solution)/shard_map/dispatch/pallas_call | solution.py:133
  8.2 0.0 copy-start.2
  8.3 0.0 copy-start
  8.3 11.2 %all-to-all-start = ((bf16[128,104,128]{2,1,0:T(8,128)(2,1)}), bf16[128,104,128]{2,1,0:T(8,128)(2,1)}, u32[]{:S(2)}, u32[]{:S(2)}) async-start(bf16[128,104,128]{2,1,0:T(8,128)(2,1)} %dispatch.1), calls=%async_computation | async-start | bytes 6815744 | tf_op jit(solution)/shard_map/all_to_all | solution.py:485
  19.5 0.0 copy-done.2
  19.5 7.6 %collective-permute-start.1 = (s32[512]{0:T(512)S(1)}, s32[512]{0:T(512)S(1)}, u32[]{:S(2)}, u32[]{:S(2)}) collective-permute-start(s32[512]{0:T(512)S(1)} %copy-done.2), channel_id=1, source_target_pairs={{1,0},{2,1},{3,2},{4,3},{5,4},{6,5},{7,6},{8,7},{9,8},{10,9},{11,1... | collective-permute-start | bytes 6152 | tf_op jit(solution)/shard_map/ppermute | solution.py:26
  27.1 1.9 %collective-permute-start = (s32[512]{0:T(512)S(1)}, s32[512]{0:T(512)S(1)}, u32[]{:S(2)}, u32[]{:S(2)}) collective-permute-start(s32[512]{0:T(512)S(1)} %copy-done.2), channel_id=1, source_target_pairs={{0,1},{1,2},{2,3},{3,4},{4,5},{5,6},{6,7},{7,8},{8,9},{9,10},{10,1... | collective-permute-start | bytes 6152 | tf_op jit(solution)/shard_map/ppermute | solution.py:26
  29.0 26.8 %collective-permute-done.1.after_tag_ref = s32[512]{0:T(512)S(1)} collective-permute-done((s32[512]{0:T(512)S(1)}, s32[512]{0:T(512)S(1)}, u32[]{:S(2)}, u32[]{:S(2)}) %collective-permute-start.1) | collective-permute-done | bytes 2080 | tf_op jit(solution)/shard_map/ppermute | solution.py:26
  55.8 4.5 %collective-permute-done.before_tag_ref = s32[512]{0:T(512)S(1)} collective-permute-done((s32[512]{0:T(512)S(1)}, s32[512]{0:T(512)S(1)}, u32[]{:S(2)}, u32[]{:S(2)}) %collective-permute-start) | collective-permute-done | bytes 2080 | tf_op jit(solution)/shard_map/ppermute | solution.py:26
  60.3 0.2 all-to-all-done.arrived_hbm
  60.5 0.0 copy-start.1
  60.5 4.2 %gather.1 = (f32[512,768]{1,0:T(8,128)S(1)}, bf16[512,768]{1,0:T(8,128)(2,1)S(1)}) custom-call(bf16[128,104,128]{2,1,0:T(8,128)(2,1)} %all-to-all-done.arrived_hbm), custom_call_target="tpu_custom_call" | custom-call | tf_op jit(solution)/shard_map/gather/pallas_call | solution.py:189
  64.7 4.8 %collective-permute-start.3 = (bf16[512,768]{1,0:T(8,128)(2,1)S(1)}, bf16[512,768]{1,0:T(8,128)(2,1)S(1)}, u32[]{:S(2)}, u32[]{:S(2)}) collective-permute-start(bf16[512,768]{1,0:T(8,128)(2,1)S(1)} %get-tuple-element.22.normed_ref), channel_id=1, source_target_pairs={{1,0},{2,1},{3,2},{4,3},{5,4},{6,5},{7,6},{8,7},{9,8},{10,9},{11,1... | collective-permute-start | bytes 2359304 | tf_op jit(solution)/shard_map/ppermute | solution.py:26
  69.5 2.1 %collective-permute-start.2 = (bf16[512,768]{1,0:T(8,128)(2,1)S(1)}, bf16[512,768]{1,0:T(8,128)(2,1)S(1)}, u32[]{:S(2)}, u32[]{:S(2)}) collective-permute-start(bf16[512,768]{1,0:T(8,128)(2,1)S(1)} %get-tuple-element.22.normed_ref), channel_id=1, source_target_pairs={{0,1},{1,2},{2,3},{3,4},{4,5},{5,6},{6,7},{7,8},{8,9},{9,10},{10,1... | collective-permute-start | bytes 2359304 | tf_op jit(solution)/shard_map/ppermute | solution.py:26
  71.6 0.0 copy-done
  71.6 0.0 copy-done.1
  71.6 11.7 %near.1 = (bf16[512,768]{1,0:T(8,128)(2,1)S(1)}, f32[512,768]{1,0:T(8,128)S(1)}, f32[512,768]{1,0:T(8,128)S(1)}, f32[512,768]{1,0:T(8,128)S(1)}, bf16[512,768]{1,0:T(8,128)(2,1)S(1)}) custom-call(s32[512]{0:T(512)S(1)} %copy-done.2, s32[512]{0:T(512)S(1)} %collective-permute-done.before_tag_ref, s32[512]{0:T(512)S(1)} %collective-permute-done.1.after_tag_ref, ...), custom_call_target="tpu_custom_call" | custom-call | tf_op jit(solution)/shard_map/near/pallas_call | solution.py:330
  83.3 3.5 %collective-permute-done.3.after_ref = bf16[512,768]{1,0:T(8,128)(2,1)S(1)} collective-permute-done((bf16[512,768]{1,0:T(8,128)(2,1)S(1)}, bf16[512,768]{1,0:T(8,128)(2,1)S(1)}, u32[]{:S(2)}, u32[]{:S(2)}) %collective-permute-start.3) | collective-permute-done | bytes 786464 | tf_op jit(solution)/shard_map/ppermute | solution.py:26
  86.8 7.7 %collective-permute-done.2.before_ref = bf16[512,768]{1,0:T(8,128)(2,1)S(1)} collective-permute-done((bf16[512,768]{1,0:T(8,128)(2,1)S(1)}, bf16[512,768]{1,0:T(8,128)(2,1)S(1)}, u32[]{:S(2)}, u32[]{:S(2)}) %collective-permute-start.2) | collective-permute-done | bytes 786464 | tf_op jit(solution)/shard_map/ppermute | solution.py:26
  94.5 16.7 %finish.1 = bf16[512,768]{1,0:T(8,128)(2,1)} custom-call(s32[512]{0:T(512)S(1)} %copy-done.2, s32[512]{0:T(512)S(1)} %collective-permute-done.before_tag_ref, s32[512]{0:T(512)S(1)} %collective-permute-done.1.after_tag_ref, s32[1,512]{1,0:T(1,128)S(1)} %bitcast.6, s32[1,512]{1,0:T(1,128)S(1)} %bitcast.8, s32[1,512]{1,0:T(1,128)S(1)} %bitcast.7, ...), custom_call_target="tpu_custom_call" | custom-call | tf_op jit(solution)/shard_map/finish/pallas_call | solution.py:450
Async XLA Ops:
  8.2 11.3 %copy-start.2 = (s32[512]{0:T(512)S(1)}, s32[512]{0:T(512)}, u32[]{:S(2)}) copy-start(s32[512]{0:T(512)} %tag_ref.1) | copy-start | bytes 6148
  8.3 63.4 %copy-start = (bf16[768,2304]{1,0:T(8,128)(2,1)S(1)}, bf16[768,2304]{1,0:T(8,128)(2,1)}, u32[]{:S(2)}) copy-start(bf16[768,2304]{1,0:T(8,128)(2,1)} %heads_ref.3) | copy-start | bytes 10616836
  8.3 52.2 %all-to-all-start = ((bf16[128,104,128]{2,1,0:T(8,128)(2,1)}), bf16[128,104,128]{2,1,0:T(8,128)(2,1)}, u32[]{:S(2)}, u32[]{:S(2)}) async-start(bf16[128,104,128]{2,1,0:T(8,128)(2,1)} %dispatch.1), calls=%async_computation | async-start | bytes 6815744 | tf_op jit(solution)/shard_map/all_to_all | solution.py:485
  19.5 36.3 %collective-permute-start.1 = (s32[512]{0:T(512)S(1)}, s32[512]{0:T(512)S(1)}, u32[]{:S(2)}, u32[]{:S(2)}) collective-permute-start(s32[512]{0:T(512)S(1)} %copy-done.2), channel_id=1, source_target_pairs={{1,0},{2,1},{3,2},{4,3},{5,4},{6,5},{7,6},{8,7},{9,8},{10,9},{11,1... | collective-permute-start | bytes 6152 | tf_op jit(solution)/shard_map/ppermute | solution.py:26
  27.1 33.3 %collective-permute-start = (s32[512]{0:T(512)S(1)}, s32[512]{0:T(512)S(1)}, u32[]{:S(2)}, u32[]{:S(2)}) collective-permute-start(s32[512]{0:T(512)S(1)} %copy-done.2), channel_id=1, source_target_pairs={{0,1},{1,2},{2,3},{3,4},{4,5},{5,6},{6,7},{7,8},{8,9},{9,10},{10,1... | collective-permute-start | bytes 6152 | tf_op jit(solution)/shard_map/ppermute | solution.py:26
  60.5 11.1 %copy-start.1 = (bf16[768,768]{1,0:T(8,128)(2,1)S(1)}, bf16[768,768]{1,0:T(8,128)(2,1)}, u32[]{:S(2)}) copy-start(bf16[768,768]{1,0:T(8,128)(2,1)} %w_out_ref.3) | copy-start | bytes 3538948
  64.7 22.1 %collective-permute-start.3 = (bf16[512,768]{1,0:T(8,128)(2,1)S(1)}, bf16[512,768]{1,0:T(8,128)(2,1)S(1)}, u32[]{:S(2)}, u32[]{:S(2)}) collective-permute-start(bf16[512,768]{1,0:T(8,128)(2,1)S(1)} %get-tuple-element.22.normed_ref), channel_id=1, source_target_pairs={{1,0},{2,1},{3,2},{4,3},{5,4},{6,5},{7,6},{8,7},{9,8},{10,9},{11,1... | collective-permute-start | bytes 2359304 | tf_op jit(solution)/shard_map/ppermute | solution.py:26
  69.5 25.1 %collective-permute-start.2 = (bf16[512,768]{1,0:T(8,128)(2,1)S(1)}, bf16[512,768]{1,0:T(8,128)(2,1)S(1)}, u32[]{:S(2)}, u32[]{:S(2)}) collective-permute-start(bf16[512,768]{1,0:T(8,128)(2,1)S(1)} %get-tuple-element.22.normed_ref), channel_id=1, source_target_pairs={{0,1},{1,2},{2,3},{3,4},{4,5},{5,6},{6,7},{7,8},{8,9},{9,10},{10,1... | collective-permute-start | bytes 2359304 | tf_op jit(solution)/shard_map/ppermute | solution.py:26
